TPU v7x, 128 devices: a whole 4x4x4 slice. The times are simulated.
128 devices in a mesh: vec: 8 (over y, z_lo), gz: 16 (over x, z_hi, core).
Axes of the slice: x: 4, y: 4, z: 4 (z_hi: 2, z_lo: 2; z = z_hi * 2 + z_lo), core: 2. Of those that a mesh axis runs over, the one named last changes fastest.
Arguments:
- vectors: bfloat16 [1024, 3, 2, 8192], P('vec', None, None, 'gz'), may hold values from -6 to 6
- links: float32 [3, 3, 3, 2, 8192], P(None, None, None, None, 'gz'), may hold values from -4 to 4
- dirs: int32 [6], replicated, may hold values from 0 to 5, each once
- moms: int32 [2, 3], replicated, may hold values from -2 to 2
Outputs:
- elementals: float32 [6, 2, 2, 1024, 1024], P(None, None, None, ('vec', 'gz'))
Inputs may be any that keep to these rules, and one draw needn't show every extreme that they name: `dirs`: each of the six directions appears exactly once.
All inputs are finite; a program needn't handle non-finite values.
Results may differ from a plain program's by a relative error of at most 0.0039.
Values may be sent and summed in bfloat16 or wider, within the bound.
A program may use at most 192 MiB of HBM per device.

v0:
```python
import math
import jax
import jax.numpy as jnp
from jax import lax
from jax.sharding import PartitionSpec as P

LX = 32
LY = 8


def colour_apply(link_real, link_imag, vec_real, vec_imag):
    out_real = jnp.float32(0.0)
    out_imag = jnp.float32(0.0)
    for column in range(3):
        left_real = link_real[None, :, column]
        left_imag = link_imag[None, :, column]
        right_real = vec_real[:, None, column].astype(jnp.float32)
        right_imag = vec_imag[:, None, column].astype(jnp.float32)
        out_real = out_real + left_real * right_real - left_imag * right_imag
        out_imag = out_imag + left_real * right_imag + left_imag * right_real
    return (out_real, out_imag)


def neighbour(field, stride, extent, position, forward):
    if forward:
        inside = jnp.roll(field, -stride, axis=-1)
        beside_all = jnp.roll(field, (extent - 1) * stride, axis=-1)
        return jnp.where(position == extent - 1, beside_all, inside)
    inside = jnp.roll(field, stride, axis=-1)
    beside_all = jnp.roll(field, -(extent - 1) * stride, axis=-1)
    return jnp.where(position == 0, beside_all, inside)


def on_device(vectors, links, dirs, moms):
    sites = vectors.shape[-1]
    plane = LY * LX
    depth = sites // plane
    shards = lax.axis_size("gz")
    flat = jnp.arange(sites, dtype=jnp.int32)
    x_index = flat % LX
    y_index = flat // LX % LY
    z_index = lax.axis_index("gz") * depth + flat // plane
    up = [(i, (i + 1) % shards) for i in range(shards)]
    down = [((i + 1) % shards, i) for i in range(shards)]
    gathered = lax.all_gather(vectors, "vec", axis=0, tiled=True)
    lower_links = lax.ppermute(links[2, :, :, :, sites - plane :], "gz", up)
    below = lax.ppermute(vectors[..., sites - plane :], "gz", up)
    above = lax.ppermute(vectors[..., :plane], "gz", down)
    momenta = moms.astype(jnp.float32)
    terms = []
    for direction in range(6):
        axis = direction % 3
        back = direction < 3
        step = -1 if back else 1
        link = links[axis]
        if axis == 0:
            moved = neighbour(vectors, 1, LX, x_index, not back)
            beside = neighbour(link, 1, LX, x_index, False) if back else link
        elif axis == 1:
            moved = neighbour(vectors, LX, LY, y_index, not back)
            beside = neighbour(link, LX, LY, y_index, False) if back else link
        elif back:
            moved = jnp.concatenate((below, vectors[..., : sites - plane]), axis=-1)
            beside = jnp.concatenate((lower_links, link[..., : sites - plane]), axis=-1)
        else:
            moved = jnp.concatenate((vectors[..., plane:], above), axis=-1)
            beside = link
        if back:
            link_real = jnp.swapaxes(beside[:, :, 0], 0, 1)
            link_imag = -jnp.swapaxes(beside[:, :, 1], 0, 1)
        else:
            link_real = beside[:, :, 0]
            link_imag = beside[:, :, 1]
        real, imag = colour_apply(link_real, link_imag, moved[:, :, 0], moved[:, :, 1])
        theta = (
            momenta[:, 0, None] * (x_index + (step if axis == 0 else 0)).astype(jnp.float32) / LX
            + momenta[:, 1, None] * (y_index + (step if axis == 1 else 0)).astype(jnp.float32) / LY
            + momenta[:, 2, None]
            * (z_index + (step if axis == 2 else 0)).astype(jnp.float32)
            / (depth * shards)
        ) * (2.0 * math.pi)
        cosine = jnp.cos(theta)[:, None, None]
        sine = jnp.sin(theta)[:, None, None]
        left_real = (cosine * real - sine * imag).astype(jnp.bfloat16)
        left_imag = (sine * real + cosine * imag).astype(jnp.bfloat16)
        left = jnp.stack(
            (jnp.stack((left_real, left_imag), axis=3), jnp.stack((-left_imag, left_real), axis=3)),
            axis=0,
        )
        product = jnp.einsum(
            "qpicrs,jcrs->pqij", left, gathered, preferred_element_type=jnp.float32
        )
        terms.append(lax.psum_scatter(product, "gz", scatter_dimension=2, tiled=True))
    stacked = jnp.stack(terms, axis=0)
    select = (dirs[:, None] == jnp.arange(6, dtype=jnp.int32)[None, :]).astype(jnp.float32)
    chosen = jnp.einsum("dk,kpqij->dpqij", select, stacked, precision=lax.Precision.HIGHEST)
    return chosen * (1.0 / math.sqrt(3.0 * sites * shards))


def solution(mesh):
    placed = (P("vec", None, None, "gz"), P(None, None, None, None, "gz"), P(), P())
    return jax.shard_map(
        on_device,
        mesh=mesh,
        in_specs=placed,
        out_specs=P(None, None, None, ("vec", "gz"), None),
        check_vma=False,
    )
```

profile of v0, /device:TPU:0, one launch (start us, length us, event | category | flops | bytes accessed | tf_op | source)
XLA Modules:
  0.0 600.4 jit_solution(9777820009141862032)
XLA Ops:
  6.5 2.1 copy.8
  8.7 2.0 fusion.148
  11.3 4.1 collective-permute-start
  18.5 1.0 fusion.129
  20.8 1.4 maximum_select_fusion
  23.7 1.4 maximum_bitcast_fusion
  27.5 1.3 maximum_select_fusion.1
  28.8 1.0 slice_bitcast_fusion.5
  29.8 110.8 %all-gather.2.cloned.1.call-done = bf16[1024,3,2,512]{3,0,2,1:T(8,128)(2,1)} async-done(((bf16[128,3,2,512]{3,0,2,1:T(8,128)(2,1)}), bf16[1024,3,2,512]{3,0,2,1:T(8,128)(2,1)}) %all-gather.2.cloned.1.call-update) | async-done | bytes 6291472 | tf_op jit(solution)/shard_map/all_gather | solution.py:45
  140.6 8.1 %fusion.30 = f32[2,2,128,1024]{3,2,0,1:T(8,128)} fusion(bf16[1024,3,2,512]{3,0,2,1:T(8,128)(2,1)} %all-gather.2.cloned.1.call-done, bf16[1,2,128,3,2,512]{5,2,4,3,1,0:T(8,128)(2,1)} %get-tuple-element.83, bf16[1,2,128,3,2,512]{5,2,4,3,1,0:T(8,128)(2,1)S(1)} %get-tuple-element.82), kind=kOutput, calls=%fused_computation.30 | convolution fusion | flops 3222798336 | bytes 11534336 | tf_op jit(solution)/shard_map/qpicrs,jcrs->pqij/dot_general | solution.py:90
  153.1 1.0 copy-done.5
  154.7 4.7 fusion.35
  161.1 1.1 fusion.64
  164.7 1.0 slice-done.3
  165.6 4.8 fusion.40
  174.5 4.8 fusion.45
  182.7 1.2 slice-done.7
  183.9 4.8 fusion.50
  188.7 4.4 collective-permute-start.2
  193.3 6.1 %collective-permute-done.2 = bf16[128,3,2,256]{3,0,2,1:T(8,128)(2,1)S(1)} collective-permute-done((bf16[128,3,2,256]{3,0,2,1:T(8,128)(2,1)S(1)}, bf16[128,3,2,256]{3,0,2,1:T(8,128)(2,1)S(1)}, u32[]{:S(2)}, u32[]{:S(2)}) %collective-permute-start.2) | collective-permute-done | bytes 393248 | tf_op jit(solution)/shard_map/ppermute | solution.py:48
  202.8 4.7 fusion.55
  207.6 13.6 %reduce-scatter.7.cloned.1.call-done = f32[2,2,8,1024]{3,2,0,1:T(8,128)} async-done(((f32[2,2,128,1024]{3,2,0,1:T(8,128)}), f32[2,2,8,1024]{3,2,0,1:T(8,128)}) %reduce-scatter.7.cloned.1.call-update) | async-done | bytes 131088 | tf_op jit(solution)/shard_map/reduce_scatter | solution.py:93
  221.2 0.9 bitcast_dynamic-update-slice_fusion.5
  222.1 73.0 %reduce-scatter.9.cloned.1.call-done = f32[2,2,8,1024]{3,2,0,1:T(8,128)} async-done(((f32[2,2,128,1024]{3,2,0,1:T(8,128)}), f32[2,2,8,1024]{3,2,0,1:T(8,128)}) %reduce-scatter.9.cloned.1.call-update) | async-done | bytes 131088 | tf_op jit(solution)/shard_map/reduce_scatter | solution.py:93
  295.1 0.9 bitcast_dynamic-update-slice_fusion.4
  296.0 72.8 %reduce-scatter.11.cloned.1.call-done = f32[2,2,8,1024]{3,2,0,1:T(8,128)} async-done(((f32[2,2,128,1024]{3,2,0,1:T(8,128)}), f32[2,2,8,1024]{3,2,0,1:T(8,128)}) %reduce-scatter.11.cloned.1.call-update) | async-done | bytes 131088 | tf_op jit(solution)/shard_map/reduce_scatter | solution.py:93
  368.9 0.9 bitcast_dynamic-update-slice_fusion.3
  369.8 72.8 %reduce-scatter.13.cloned.1.call-done = f32[2,2,8,1024]{3,2,0,1:T(8,128)} async-done(((f32[2,2,128,1024]{3,2,0,1:T(8,128)}), f32[2,2,8,1024]{3,2,0,1:T(8,128)}) %reduce-scatter.13.cloned.1.call-update) | async-done | bytes 131088 | tf_op jit(solution)/shard_map/reduce_scatter | solution.py:93
  443.5 72.8 %reduce-scatter.15.cloned.1.call-done = f32[2,2,8,1024]{3,2,0,1:T(8,128)} async-done(((f32[2,2,128,1024]{3,2,0,1:T(8,128)}), f32[2,2,8,1024]{3,2,0,1:T(8,128)}) %reduce-scatter.15.cloned.1.call-update) | async-done | bytes 131088 | tf_op jit(solution)/shard_map/reduce_scatter | solution.py:93
  517.3 73.0 %reduce-scatter.17.cloned.1.call-done = f32[2,2,8,1024]{3,2,0,1:T(8,128)} async-done(((f32[2,2,128,1024]{3,2,0,1:T(8,128)}), f32[2,2,8,1024]{3,2,0,1:T(8,128)}) %reduce-scatter.17.cloned.1.call-update) | async-done | bytes 131088 | tf_op jit(solution)/shard_map/reduce_scatter | solution.py:93
  591.2 1.0 convolution_multiply_fusion
  592.2 1.3 copy.28
  (220 shorter events, 31.1 us)
Async XLA Ops:
  6.5 134.0 %all-gather.2.cloned.1.call-start = ((), (), s32[]{:S(2)}) async-start(), calls=%async_computation.6 | async-start | bytes 7077888 | tf_op jit(solution)/shard_map/all_gather | solution.py:45
  8.6 9.6 %copy-start.29 = (s32[2,3]{1,0:T(2,128)S(1)}, s32[2,3]{1,0:T(2,128)}, u32[]{:S(2)}) copy-start(s32[2,3]{1,0:T(2,128)} %param.7) | copy-start | bytes 76
  8.6 11.1 %copy-start = (bf16[128,3,2,512]{3,0,2,1:T(8,128)(2,1)S(1)}, bf16[128,3,2,512]{3,0,2,1:T(8,128)(2,1)}, u32[]{:S(2)}) copy-start(bf16[128,3,2,512]{3,0,2,1:T(8,128)(2,1)} %copy.8) | copy-start | bytes 2359300
  8.7 212.5 %reduce-scatter.7.cloned.1.call-start = ((), (), s32[]{:S(2)}) async-start(), calls=%async_computation.7 | async-start | bytes 2228224 | tf_op jit(solution)/shard_map/reduce_scatter | solution.py:93
  10.7 150.4 %collective-permute-start.1 = (bf16[128,3,2,256]{3,0,2,1:T(8,128)(2,1)S(1)}, bf16[128,3,2,256]{3,0,2,1:T(8,128)(2,1)}, u32[]{:S(2)}, u32[]{:S(2)}) collective-permute-start(bf16[128,3,2,256]{3,0,2,1:T(8,128)(2,1)S(1)} %get-tuple-element.76), channel_id=1, source_target_pairs={{0,1},{1,2},{2,3},{3,4},{4,5},{5,6},{6,7},{7,8},{8,9},{9,10},{10,1... | collective-permute-start | bytes 1179656 | tf_op jit(solution)/shard_map/ppermute | solution.py:47
  11.3 148.2 %collective-permute-start = (f32[3,3,2,256]{3,2,1,0:T(2,128)}, f32[3,3,2,256]{3,2,1,0:T(2,128)}, u32[]{:S(2)}, u32[]{:S(2)}) collective-permute-start(f32[3,3,2,256]{3,2,1,0:T(2,128)} %slice_bitcast_fusion.47), channel_id=1, source_target_pairs={{0,1},{1,2},{2,3},{3,4},{4,5},{5,6},{6,7},{7,8},{8,9},{9,10},{10,1... | collective-permute-start | bytes 55304 | tf_op jit(solution)/shard_map/ppermute | solution.py:46
  16.0 4.4 copy-start.4
  16.0 4.4 copy-start.6
  23.7 2.2 copy-start.8
  148.7 2.7 copy-start.27
  148.7 2.7 copy-start.12
  148.7 2.7 copy-start.3
  148.7 2.8 copy-start.2
  148.7 146.4 %reduce-scatter.9.cloned.1.call-start = ((), (), s32[]{:S(2)}) async-start(), calls=%async_computation.8 | async-start | bytes 2228224 | tf_op jit(solution)/shard_map/reduce_scatter | solution.py:93
  151.6 2.6 slice-start
  159.5 209.4 %reduce-scatter.11.cloned.1.call-start = ((), (), s32[]{:S(2)}) async-start(), calls=%async_computation.9 | async-start | bytes 2228224 | tf_op jit(solution)/shard_map/reduce_scatter | solution.py:93
  162.4 2.3 slice-start.2
  163.3 2.3 slice-start.3
  170.5 272.1 %reduce-scatter.13.cloned.1.call-start = ((), (), s32[]{:S(2)}) async-start(), calls=%async_computation.10 | async-start | bytes 2228224 | tf_op jit(solution)/shard_map/reduce_scatter | solution.py:93
  171.4 2.2 slice-start.4
  172.3 2.2 slice-start.5
  179.3 337.0 %reduce-scatter.15.cloned.1.call-start = ((), (), s32[]{:S(2)}) async-start(), calls=%async_computation.11 | async-start | bytes 2228224 | tf_op jit(solution)/shard_map/reduce_scatter | solution.py:93
  180.5 2.2 slice-start.6
  181.4 2.5 slice-start.7
  188.6 4.4 copy-start.16
  188.6 4.5 copy-start.15
  188.6 4.6 copy-start.24
  188.7 401.6 %reduce-scatter.17.cloned.1.call-start = ((), (), s32[]{:S(2)}) async-start(), calls=%async_computation.12 | async-start | bytes 2228224 | tf_op jit(solution)/shard_map/reduce_scatter | solution.py:93
  188.7 10.7 %collective-permute-start.2 = (bf16[128,3,2,256]{3,0,2,1:T(8,128)(2,1)S(1)}, bf16[128,3,2,256]{3,0,2,1:T(8,128)(2,1)S(1)}, u32[]{:S(2)}, u32[]{:S(2)}) collective-permute-start(bf16[128,3,2,256]{3,0,2,1:T(8,128)(2,1)S(1)} %copy-done.1), channel_id=1, source_target_pairs={{1,0},{2,1},{3,2},{4,3},{5,4},{6,5},{7,6},{8,7},{9,8},{10,9},{11,1... | collective-permute-start | bytes 1179656 | tf_op jit(solution)/shard_map/ppermute | solution.py:48
  199.7 2.2 slice-start.8
  200.6 2.2 slice-start.9
  207.5 383.6 %copy-start.30 = (s32[6]{0:T(128)S(1)}, s32[6]{0:T(128)}, u32[]{:S(2)}) copy-start(s32[6]{0:T(128)} %param.6) | copy-start | bytes 76
  (19 other events, 22.8 us)
Sparse Core Ops, SparseCore 0:
  9.0 131.5 all-gather.1
  148.8 72.2 reduce-scatter.6
  225.1 69.9 reduce-scatter.8
  298.9 69.9 reduce-scatter.10
  372.7 69.9 reduce-scatter.12
  446.4 69.9 reduce-scatter.14
  520.3 69.8 reduce-scatter.16
where the time goes:
time: 601 us; the launch traced here: 600 us
  waiting for transfers between devices  495 us (82%)
  matrix products  32.9 us (5%)
  local copies, waits for them, and re-layouts  32.3 us (5%)
  other arithmetic  16.4 us (3%)
  between operations  14.6 us (2%)
  starting transfers between devices  9.11 us (2%)
    reduce_scatter x6, waiting for transfers between devices, on_device(): lax.psum_scatter(product, 'gz', scatter_dimension=2, tiled=True)  378 us
    all_gather x1, waiting for transfers between devices, on_device(): gathered = lax.all_gather(vectors, 'vec', axis=0, tiled=True)  111 us
    dot_general x6, matrix products, on_device(): jnp.einsum('qpicrs,jcrs->pqij', left, gathered, preferred_element_type=jn...  31.9 us
    unnamed x111, local copies, waits for them, and re-layouts  18.3 us
  transfers between devices with their start and end apart: 10, of which 8 were waited for; matrix products, arithmetic and copies ran while one was open for 11% of the time, Pallas kernels for 0%

commit v1 on v0

--- a/solution.py
+++ b/solution.py
@@ -42,7 +42,9 @@
     z_index = lax.axis_index("gz") * depth + flat // plane
     up = [(i, (i + 1) % shards) for i in range(shards)]
     down = [((i + 1) % shards, i) for i in range(shards)]
-    gathered = lax.all_gather(vectors, "vec", axis=0, tiled=True)
+    gathered = jnp.concatenate(
+        lax.all_to_all(jnp.stack([vectors] * lax.axis_size("vec")), "vec", 0, 0), axis=0
+    )
     lower_links = lax.ppermute(links[2, :, :, :, sites - plane :], "gz", up)
     below = lax.ppermute(vectors[..., sites - plane :], "gz", up)
     above = lax.ppermute(vectors[..., :plane], "gz", down)

time: 601 us -> 572 us (0.952)
  waiting for transfers between devices: 495 us -> 446 us
  starting transfers between devices: 9.11 us -> 19 us
  local copies, waits for them, and re-layouts: 32.3 us -> 41.8 us
    all_gather x1 -> x0, waiting for transfers between devices: 111 us -> none  [on_device(): gathered = lax.all_gather(vectors, 'vec', axis=0, tiled=True)]
    all_to_all x0 -> x1, waiting for transfers between devices: none -> 68.2 us  [on_device(): lax.all_to_all(jnp.stack([vectors] * lax.axis_size('vec')), 'vec', 0, 0)]
    unnamed x111 -> x107, local copies, waits for them, and re-layouts: 18.3 us -> 21.5 us
  transfers between devices with their start and end apart: 10 -> 10, of which waited for: 8 -> 8; matrix products, arithmetic and copies ran while one was open for 11% -> 12% of each run, Pallas kernels for 0% -> 0%
where the time goes in v1:
time: 572 us; the launch traced here: 571 us
  waiting for transfers between devices  446 us (78%)
  local copies, waits for them, and re-layouts  41.8 us (7%)
  matrix products  29.7 us (5%)
  other arithmetic  19.4 us (3%)
  starting transfers between devices  19 us (3%)
  between operations  14.5 us (3%)
    reduce_scatter x6, waiting for transfers between devices, on_device(): lax.psum_scatter(product, 'gz', scatter_dimension=2, tiled=True)  373 us
    all_to_all x1, waiting for transfers between devices, on_device(): lax.all_to_all(jnp.stack([vectors] * lax.axis_size('vec')), 'vec', 0, 0)  68.2 us
    dot_general x6, matrix products, on_device(): jnp.einsum('qpicrs,jcrs->pqij', left, gathered, preferred_element_type=jn...  28.6 us
    unnamed x107, local copies, waits for them, and re-layouts  21.5 us
  transfers between devices with their start and end apart: 10, of which 8 were waited for; matrix products, arithmetic and copies ran while one was open for 12% of the time, Pallas kernels for 0%

profile of v1, /device:TPU:0, one launch (start us, length us, event | category | flops | bytes accessed | tf_op | source)
XLA Modules:
  0.0 570.8 jit_solution(6875869718207664601)
XLA Ops:
  6.5 1.2 copy.29
  7.8 3.5 stack.151
  11.2 5.9 %all-to-all-start = ((bf16[8,128,3,2,512]{4,1,3,2,0:T(8,128)(2,1)}), bf16[8,128,3,2,512]{4,1,3,2,0:T(8,128)(2,1)}, u32[]{:S(2)}, u32[]{:S(2)}) async-start(bf16[8,128,3,2,512]{4,1,3,2,0:T(8,128)(2,1)} %stack.151), calls=%async_computation | async-start | bytes 12582912 | tf_op jit(solution)/shard_map/all_to_all | solution.py:46
  17.2 1.0 fusion.130
  18.8 3.7 collective-permute-start
  24.2 1.0 fusion.111
  26.0 1.4 maximum_select_fusion
  28.9 1.8 maximum_bitcast_fusion
  35.1 1.3 fusion.125
  36.7 68.2 %all-to-all-done = bf16[8,128,3,2,512]{4,1,3,2,0:T(8,128)(2,1)} async-done(((bf16[8,128,3,2,512]{4,1,3,2,0:T(8,128)(2,1)}), bf16[8,128,3,2,512]{4,1,3,2,0:T(8,128)(2,1)}, u32[]{:S(2)}, u32[]{:S(2)}) %all-to-all-start) | async-done | bytes 6291488 | tf_op jit(solution)/shard_map/all_to_all | solution.py:46
  104.9 3.7 copy.34
  108.6 2.6 copy-done
  111.2 4.8 fusion.39
  118.7 2.6 maximum_select_fusion.1
  125.2 4.7 fusion.36
  131.6 1.1 fusion.46
  136.2 4.8 fusion.33
  145.8 4.7 fusion.30
  153.9 1.0 slice-done.7
  154.9 4.8 fusion.27
  159.8 8.8 %collective-permute-start.2 = (bf16[128,3,2,256]{3,0,2,1:T(8,128)(2,1)S(1)}, bf16[128,3,2,256]{3,0,2,1:T(8,128)(2,1)S(1)}, u32[]{:S(2)}, u32[]{:S(2)}) collective-permute-start(bf16[128,3,2,256]{3,0,2,1:T(8,128)(2,1)S(1)} %copy-done.3), channel_id=1, source_target_pairs={{1,0},{2,1},{3,2},{4,3},{5,4},{6,5},{7,6},{8,7},{9,8},{10,9},{11,1... | collective-permute-start | bytes 1179656 | tf_op jit(solution)/shard_map/ppermute | solution.py:50
  168.8 5.1 collective-permute-done.2
  173.8 1.1 fusion.44
  178.2 4.7 fusion.24
  183.0 9.0 %reduce-scatter.7.cloned.1.call-done = f32[2,2,8,1024]{3,2,0,1:T(8,128)} async-done(((f32[2,2,128,1024]{3,2,0,1:T(8,128)}), f32[2,2,8,1024]{3,2,0,1:T(8,128)}) %reduce-scatter.7.cloned.1.call-update) | async-done | bytes 131088 | tf_op jit(solution)/shard_map/reduce_scatter | solution.py:95
  192.9 73.0 %reduce-scatter.9.cloned.1.call-done = f32[2,2,8,1024]{3,2,0,1:T(8,128)} async-done(((f32[2,2,128,1024]{3,2,0,1:T(8,128)}), f32[2,2,8,1024]{3,2,0,1:T(8,128)}) %reduce-scatter.9.cloned.1.call-update) | async-done | bytes 131088 | tf_op jit(solution)/shard_map/reduce_scatter | solution.py:95
  266.8 72.9 %reduce-scatter.11.cloned.1.call-done = f32[2,2,8,1024]{3,2,0,1:T(8,128)} async-done(((f32[2,2,128,1024]{3,2,0,1:T(8,128)}), f32[2,2,8,1024]{3,2,0,1:T(8,128)}) %reduce-scatter.11.cloned.1.call-update) | async-done | bytes 131088 | tf_op jit(solution)/shard_map/reduce_scatter | solution.py:95
  340.6 72.8 %reduce-scatter.13.cloned.1.call-done = f32[2,2,8,1024]{3,2,0,1:T(8,128)} async-done(((f32[2,2,128,1024]{3,2,0,1:T(8,128)}), f32[2,2,8,1024]{3,2,0,1:T(8,128)}) %reduce-scatter.13.cloned.1.call-update) | async-done | bytes 131088 | tf_op jit(solution)/shard_map/reduce_scatter | solution.py:95
  414.3 72.7 %reduce-scatter.15.cloned.1.call-done = f32[2,2,8,1024]{3,2,0,1:T(8,128)} async-done(((f32[2,2,128,1024]{3,2,0,1:T(8,128)}), f32[2,2,8,1024]{3,2,0,1:T(8,128)}) %reduce-scatter.15.cloned.1.call-update) | async-done | bytes 131088 | tf_op jit(solution)/shard_map/reduce_scatter | solution.py:95
  487.9 72.8 %reduce-scatter.17.cloned.1.call-done = f32[2,2,8,1024]{3,2,0,1:T(8,128)} async-done(((f32[2,2,128,1024]{3,2,0,1:T(8,128)}), f32[2,2,8,1024]{3,2,0,1:T(8,128)}) %reduce-scatter.17.cloned.1.call-update) | async-done | bytes 131088 | tf_op jit(solution)/shard_map/reduce_scatter | solution.py:95
  561.6 1.0 convolution_multiply_fusion
  562.7 1.3 copy.50
  (217 shorter events, 37.3 us)
Async XLA Ops:
  11.2 93.7 %all-to-all-start = ((bf16[8,128,3,2,512]{4,1,3,2,0:T(8,128)(2,1)}), bf16[8,128,3,2,512]{4,1,3,2,0:T(8,128)(2,1)}, u32[]{:S(2)}, u32[]{:S(2)}) async-start(bf16[8,128,3,2,512]{4,1,3,2,0:T(8,128)(2,1)} %stack.151), calls=%async_computation | async-start | bytes 12582912 | tf_op jit(solution)/shard_map/all_to_all | solution.py:46
  17.2 174.8 %reduce-scatter.7.cloned.1.call-start = ((), (), s32[]{:S(2)}) async-start(), calls=%async_computation.7 | async-start | bytes 2228224 | tf_op jit(solution)/shard_map/reduce_scatter | solution.py:95
  18.2 5.9 %copy-start.27 = (s32[2,3]{1,0:T(2,128)S(1)}, s32[2,3]{1,0:T(2,128)}, u32[]{:S(2)}) copy-start(s32[2,3]{1,0:T(2,128)} %param.7) | copy-start | bytes 76
  18.2 113.4 %collective-permute-start.1 = (bf16[128,3,2,256]{3,0,2,1:T(8,128)(2,1)}, bf16[128,3,2,256]{3,0,2,1:T(8,128)(2,1)}, u32[]{:S(2)}, u32[]{:S(2)}) collective-permute-start(bf16[128,3,2,256]{3,0,2,1:T(8,128)(2,1)} %get-tuple-element.76), channel_id=1, source_target_pairs={{0,1},{1,2},{2,3},{3,4},{4,5},{5,6},{6,7},{7,8},{8,9},{9,10},{10,1... | collective-permute-start | bytes 1179656 | tf_op jit(solution)/shard_map/ppermute | solution.py:49
  18.8 111.2 %collective-permute-start = (f32[3,3,2,256]{3,2,1,0:T(2,128)}, f32[3,3,2,256]{3,2,1,0:T(2,128)}, u32[]{:S(2)}, u32[]{:S(2)}) collective-permute-start(f32[3,3,2,256]{3,2,1,0:T(2,128)} %slice_bitcast_fusion.47), channel_id=1, source_target_pairs={{0,1},{1,2},{2,3},{3,4},{4,5},{5,6},{6,7},{7,8},{8,9},{9,10},{10,1... | collective-permute-start | bytes 55304 | tf_op jit(solution)/shard_map/ppermute | solution.py:48
  23.4 7.3 %copy-start.4 = (f32[3,3,2,512]{3,2,1,0:T(2,128)}, f32[3,3,2,512]{3,2,1,0:T(2,128)S(1)}, u32[]{:S(2)}) copy-start(f32[3,3,2,512]{3,2,1,0:T(2,128)S(1)} %get-tuple-element.123) | copy-start | bytes 110596
  23.6 7.1 %copy-start.26 = (pred[512]{0:T(512)(128)(4,1)}, pred[512]{0:T(512)(128)(4,1)S(1)}, u32[]{:S(2)}) copy-start(pred[512]{0:T(512)(128)(4,1)S(1)} %broadcast_compare_fusion.1) | copy-start | bytes 1540
  104.9 6.3 %copy-start.1 = (bf16[1,2,128,3,2,512]{5,2,4,3,1,0:T(8,128)(2,1)S(1)}, bf16[1,2,128,3,2,512]{5,2,4,3,1,0:T(8,128)(2,1)}, u32[]{:S(2)}) copy-start(bf16[1,2,128,3,2,512]{5,2,4,3,1,0:T(8,128)(2,1)} %get-tuple-element.82) | copy-start | bytes 4718596
  104.9 6.3 %copy-start.2 = (bf16[1,2,128,3,2,512]{5,2,4,3,1,0:T(8,128)(2,1)S(1)}, bf16[1,2,128,3,2,512]{5,2,4,3,1,0:T(8,128)(2,1)}, u32[]{:S(2)}) copy-start(bf16[1,2,128,3,2,512]{5,2,4,3,1,0:T(8,128)(2,1)} %get-tuple-element.83) | copy-start | bytes 4718596
  108.6 2.6 copy-start
  116.0 1.4 copy-start.24
  116.0 2.1 copy-start.20
  116.0 149.8 %reduce-scatter.9.cloned.1.call-start = ((), (), s32[]{:S(2)}) async-start(), calls=%async_computation.8 | async-start | bytes 2228224 | tf_op jit(solution)/shard_map/reduce_scatter | solution.py:95
  121.5 1.2 copy-start.12
  122.1 2.2 slice-start
  123.0 2.2 slice-start.1
  129.9 1.6 copy-start.3
  130.0 209.7 %reduce-scatter.11.cloned.1.call-start = ((), (), s32[]{:S(2)}) async-start(), calls=%async_computation.9 | async-start | bytes 2228224 | tf_op jit(solution)/shard_map/reduce_scatter | solution.py:95
  132.9 2.3 slice-start.2
  133.8 2.4 slice-start.3
  141.0 272.3 %reduce-scatter.13.cloned.1.call-start = ((), (), s32[]{:S(2)}) async-start(), calls=%async_computation.10 | async-start | bytes 2228224 | tf_op jit(solution)/shard_map/reduce_scatter | solution.py:95
  142.8 2.2 slice-start.4
  143.6 2.2 slice-start.5
  150.6 336.4 %reduce-scatter.15.cloned.1.call-start = ((), (), s32[]{:S(2)}) async-start(), calls=%async_computation.11 | async-start | bytes 2228224 | tf_op jit(solution)/shard_map/reduce_scatter | solution.py:95
  151.6 2.3 slice-start.6
  152.5 2.5 slice-start.7
  159.7 9.0 %copy-start.21 = (f32[2,512]{1,0:T(2,128)S(1)}, f32[2,512]{1,0:T(2,128)}, u32[]{:S(2)}) copy-start(f32[2,512]{1,0:T(2,128)} %get-tuple-element.11) | copy-start | bytes 12292
  159.7 400.9 %reduce-scatter.17.cloned.1.call-start = ((), (), s32[]{:S(2)}) async-start(), calls=%async_computation.12 | async-start | bytes 2228224 | tf_op jit(solution)/shard_map/reduce_scatter | solution.py:95
  159.8 14.0 %collective-permute-start.2 = (bf16[128,3,2,256]{3,0,2,1:T(8,128)(2,1)S(1)}, bf16[128,3,2,256]{3,0,2,1:T(8,128)(2,1)S(1)}, u32[]{:S(2)}, u32[]{:S(2)}) collective-permute-start(bf16[128,3,2,256]{3,0,2,1:T(8,128)(2,1)S(1)} %copy-done.3), channel_id=1, source_target_pairs={{1,0},{2,1},{3,2},{4,3},{5,4},{6,5},{7,6},{8,7},{9,8},{10,9},{11,1... | collective-permute-start | bytes 1179656 | tf_op jit(solution)/shard_map/ppermute | solution.py:50
  175.1 2.2 slice-start.8
  176.0 2.2 slice-start.9
  183.0 378.6 %copy-start.28 = (s32[6]{0:T(128)S(1)}, s32[6]{0:T(128)}, u32[]{:S(2)}) copy-start(s32[6]{0:T(128)} %param.6) | copy-start | bytes 76
  (17 other events, 13.3 us)
Sparse Core Ops, SparseCore 0:
  116.1 75.7 reduce-scatter.6
  195.9 69.8 reduce-scatter.8
  269.8 69.8 reduce-scatter.10
  343.5 69.8 reduce-scatter.12
  417.1 69.8 reduce-scatter.14
  490.8 69.8 reduce-scatter.16
